TPU v7x, 256 devices: a whole 4x4x8 slice. The times are simulated.
256 devices in a mesh: section: 4 (over x), shard: 64 (over z, y, core).
Axes of the slice: x: 4, y: 4, z: 8, core: 2. Of those that a mesh axis runs over, the one named last changes fastest.
Arguments:
- voltages: bfloat16 [4, 2, 1024, 32768], P('section', None, 'shard'), may hold values from -30 to 30, as said below
- feed_gains: bfloat16 [2, 1024, 1024], P(None, 'shard'), may hold values from -6 to 6
- grid_index: int32 [1024], replicated, may hold values from 0 to 1023, each once
- decay_rates: float32 [1024], P('shard'), may hold values from 0.3 to 0.95
- delays: int32 [1024, 512], replicated, may hold values from 0 to 4095
Outputs:
- dedispersed: bfloat16 [4, 7, 512, 2, 1024], P('section', None, None, None, 'shard')
Inputs may be any that keep to these rules, and one draw needn't show every extreme that they name: Real sample voltages.
All inputs are finite; a program needn't handle non-finite values.
Results may differ from a plain program's by a relative error of at most 0.009.
Values may be sent and summed in bfloat16 or wider, within the bound.
A program may use at most 192 MiB of HBM per device.

v0:
```python
import math
import jax
import jax.numpy as jnp
import numpy as np
from jax import lax
from jax.sharding import PartitionSpec as P

POL = 2
GRID_X = 4
GRID_Y = 256
NSAMP = 2048
TDFT = 16
FEEDS = 1024
CHANS = 1024
MODF = 7


def carried_in(part, axis, combine, identity):
    place = lax.axis_index(axis)
    gathered = jax.tree.map(lambda a: lax.all_gather(a, axis), part)
    state = jax.tree.map(lambda a, e: jnp.zeros_like(a) + jnp.asarray(e, a.dtype), part, identity)

    def one(lap, state):
        return combine(
            state, jax.tree.map(lambda a: lax.dynamic_index_in_dim(a, lap, 0, False), gathered)
        )

    return lax.fori_loop(0, place, one, state)


def spectral_constant():
    row_index = np.arange(CHANS, dtype=np.int64)[:, None]
    col_index = np.arange(NSAMP, dtype=np.int64)[None, :]
    angles = np.float32(2.0 * math.pi / NSAMP) * (row_index * col_index % NSAMP).astype(np.float32)
    table = np.concatenate([np.cos(angles), -np.sin(angles)], 0).astype(np.float32)
    return jnp.asarray(table).astype(jnp.bfloat16)


def twiddle_table(length):
    row_index = jnp.arange(length, dtype=jnp.int32)[:, None]
    col_index = jnp.arange(length, dtype=jnp.int32)[None, :]
    angles = 2.0 * math.pi / length * (row_index * col_index % length).astype(jnp.float32)
    cosine = jnp.cos(angles)
    sine_part = jnp.sin(angles)
    return jnp.stack([jnp.stack([cosine, -sine_part], 1), jnp.stack([sine_part, cosine], 1)], 0)


def frame_table():
    frames = jnp.arange(TDFT, dtype=jnp.int32)[:, None]
    freqs = jnp.arange(1, MODF + 1, dtype=jnp.int32)[None, :]
    angles = 2.0 * math.pi / TDFT * (frames * freqs % TDFT).astype(jnp.float32)
    return jnp.concatenate([jnp.cos(angles), -jnp.sin(angles)], 1) / math.sqrt(TDFT)


def form_beams(transposed_block, feed_gains, cell_feed):
    chan_count = transposed_block.shape[1]
    pol_count = transposed_block.shape[2]
    values = transposed_block.reshape(2, chan_count, pol_count, FEEDS, TDFT).astype(jnp.float32)
    gain_values = feed_gains.astype(jnp.float32)[:, :, None, :, None]
    real_part = gain_values[0] * values[0] - gain_values[1] * values[1]
    imag_part = gain_values[0] * values[1] + gain_values[1] * values[0]
    calibrated = jnp.stack([real_part, imag_part]).astype(jnp.bfloat16)
    gridded = jnp.take(calibrated, cell_feed, axis=3).reshape(
        2, chan_count, pol_count, GRID_X, GRID_Y, TDFT
    )
    rows = twiddle_table(GRID_Y).astype(jnp.bfloat16)
    row_beams = jnp.einsum("acpxyn,aybw->bcpxwn", gridded, rows, preferred_element_type=jnp.float32)
    beam_voltage = jnp.einsum(
        "bcpxwn,bxeu->ecpnuw", row_beams, twiddle_table(GRID_X), precision=lax.Precision.HIGHEST
    )
    powers = jnp.sum(beam_voltage * beam_voltage, axis=0)
    return jnp.moveaxis(powers, 1, 0).reshape(pol_count, chan_count, TDFT, FEEDS)


def dedisperse(freq_major, delays):
    residues = delays % TDFT
    contract = (((0,), (0,)), ((), ()))

    def per_frequency(position_index):
        frequency = position_index + 1
        angles = 2.0 * math.pi / TDFT * (frequency * residues % TDFT).astype(jnp.float32)
        cosine_part = jnp.cos(angles).astype(jnp.bfloat16)
        sine_part = jnp.sin(angles).astype(jnp.bfloat16)
        mod_real = freq_major[position_index]
        mod_imag = freq_major[MODF + position_index]
        real_out = lax.dot_general(
            cosine_part, mod_real, contract, preferred_element_type=jnp.float32
        ) + lax.dot_general(sine_part, mod_imag, contract, preferred_element_type=jnp.float32)
        imag_out = lax.dot_general(
            cosine_part, mod_imag, contract, preferred_element_type=jnp.float32
        ) - lax.dot_general(sine_part, mod_real, contract, preferred_element_type=jnp.float32)
        result = jnp.stack([real_out, imag_out], 1) / math.sqrt(CHANS)
        return result.astype(jnp.bfloat16)

    return lax.map(per_frequency, jnp.arange(MODF, dtype=jnp.int32))


def combine(earlier, later):
    return (
        earlier[0] * later[0],
        later[0] * earlier[1] + later[1],
        later[0] * earlier[2] + later[2],
    )


def shards(voltages, feed_gains, grid_index, decay_rates, delays):
    cell_feed = (
        jnp.zeros((FEEDS,), jnp.int32).at[grid_index].set(jnp.arange(FEEDS, dtype=jnp.int32))
    )
    local_feeds = voltages.shape[2]
    samples = voltages[0].reshape(POL * local_feeds * TDFT, NSAMP)
    spectra = lax.dot_general(
        spectral_constant(), samples, (((1,), (1,)), ((), ())), preferred_element_type=jnp.float32
    )
    spectra = (
        (spectra * (1.0 / math.sqrt(NSAMP)))
        .astype(jnp.bfloat16)
        .reshape(2, CHANS, POL, local_feeds * TDFT)
    )
    turned = lax.all_to_all(spectra, "shard", split_axis=1, concat_axis=3, tiled=True)
    per_pol = form_beams(turned, feed_gains, cell_feed)
    beam_power = jnp.sum(per_pol, axis=0)
    levels = jnp.mean(beam_power, axis=(1, 2)) + 1e-06
    unity = jnp.ones_like(levels)
    nothing = jnp.zeros_like(levels)
    prefix = carried_in((decay_rates, levels, unity), "section", combine, (unity, nothing, nothing))
    baseline_level = (decay_rates * prefix[1] + levels) / (decay_rates * prefix[2] + 1.0)
    normalized = beam_power / baseline_level[:, None, None] - 1.0
    modulated = jnp.einsum(
        "cnb,nq->cbq", normalized, frame_table(), precision=lax.Precision.HIGHEST
    ).astype(jnp.bfloat16)
    flattened = modulated.reshape(modulated.shape[0], FEEDS * 2 * MODF)
    moved = lax.all_to_all(flattened, "shard", split_axis=1, concat_axis=0, tiled=True)
    local_beams = FEEDS // lax.axis_size("shard")
    gathered = moved.reshape(CHANS, local_beams, 2 * MODF)
    freq_major = jnp.transpose(gathered, (2, 0, 1))
    return dedisperse(freq_major, delays)[None]


def solution(mesh):
    in_specs = (P("section", None, "shard", None), P(None, "shard", None), P(), P("shard"), P())
    out_specs = P("section", None, None, None, "shard")
    return jax.shard_map(shards, mesh=mesh, in_specs=in_specs, out_specs=out_specs, check_vma=False)
```

profile of v0, /device:TPU:1, one launch (start us, length us, event | category | flops | bytes accessed | tf_op | source)
XLA Modules:
  0.0 509.6 jit_solution(17534313984835223672)
XLA Ops:
  2.9 9.2 %multiply_convert_fusion = bf16[2048,512]{1,0:T(8,128)(2,1)} fusion(bf16[2048,2048]{1,0:T(8,128)(2,1)} %constant.189, bf16[512,2048]{1,0:T(8,128)(2,1)S(1)} %reshape_squeeze.3), kind=kOutput, calls=%fused_computation.43 | convolution fusion | flops 4297064448 | bytes 12582912 | tf_op jit(solution)/shard_map/dot_general | solution.py:112
  17.4 13.3 %all-to-all-start = ((bf16[2,1024,2,256]{3,2,0,1:T(2,128)(2,1)}), bf16[2,1024,2,256]{3,2,0,1:T(2,128)(2,1)S(1)}, u32[]{:S(2)}, u32[]{:S(2)}) async-start(bf16[2,1024,2,256]{3,2,0,1:T(2,128)(2,1)} %copy.40), calls=%async_computation | async-start | bytes 4194304 | tf_op jit(solution)/shard_map/all_to_all | solution.py:120
  40.5 39.9 %all-to-all-done = bf16[2,1024,2,256]{3,2,0,1:T(2,128)(2,1)S(1)} async-done(((bf16[2,1024,2,256]{3,2,0,1:T(2,128)(2,1)}), bf16[2,1024,2,256]{3,2,0,1:T(2,128)(2,1)S(1)}, u32[]{:S(2)}, u32[]{:S(2)}) %all-to-all-start) | async-done | bytes 2097184 | tf_op jit(solution)/shard_map/all_to_all | solution.py:120
  84.5 8.6 %slice.26 = f32[1,16,2,1024,16]{4,3,2,1,0:T(8,128)} reshape(f32[1,16,2,64,256]{4,3,2,1,0:T(8,128)S(1)} %copy.42) | data formatting | bytes 4194304 | tf_op jit(solution)/shard_map/slice | solution.py:60
  95.9 8.6 %slice.29 = f32[1,16,2,1024,16]{4,3,2,1,0:T(8,128)} reshape(f32[1,16,2,64,256]{4,3,2,1,0:T(8,128)S(1)} %copy.43) | data formatting | bytes 4194304 | tf_op jit(solution)/shard_map/slice | solution.py:60
  104.5 18.1 %multiply_subtract_fusion = (bf16[1,16,2,1024,16]{4,3,2,1,0:T(8,128)(2,1)}, bf16[1,16,2,1024,16]{4,3,2,1,0:T(8,128)(2,1)}) fusion(f32[1,16,2,1024,16]{4,3,2,1,0:T(8,128)} %slice.29, f32[1,16,2,1024,16]{4,3,2,1,0:T(8,128)} %slice.26, f32[16,1024]{1,0:T(8,128)S(1)} %get-tuple-element.203, f32[16,1024]{1,0:T(8,128)S(1)} %get-tuple-element.202), kind=kLoop, calls=%fused_computation.37 | loop fusion | flops 4194304 | bytes 6422528 | tf_op jit(solution)/shard_map/sub | solution.py:60
  129.2 7.8 %copy.45 = bf16[1,16,2,1024,16]{3,4,2,1,0:T(8,128)(2,1)} copy(bf16[1,16,2,1024,16]{4,3,2,1,0:T(8,128)(2,1)} %get-tuple-element.197) | data formatting | bytes 2097152 | tf_op jit(solution)/shard_map/add | solution.py:61
  138.4 16.1 %copy.46 = bf16[2,16,2,1024,16]{4,1,3,2,0:T(8,128)(2,1)} copy(bf16[2,16,2,1024,16]{3,4,2,1,0:T(8,128)(2,1)S(1)} %pad_maximum_fusion) | data formatting | bytes 4194304 | tf_op jit(solution)/shard_map/stack | solution.py:62
  154.5 20.1 %gather_fusion = bf16[1024,2,16,2,16]{4,2,3,1,0:T(8,128)(2,1)} fusion(bf16[2,16,2,1024,16]{4,1,3,2,0:T(8,128)(2,1)} %copy.46, s32[1024]{0:T(1024)S(1)} %fusion.59), kind=kCustom, calls=%fused_computation | custom fusion | bytes 4198400 | tf_op jit(solution)/shard_map/jit(_take)/gather | solution.py:63
  174.7 17.1 %copy.47 = bf16[2,16,2,4,256,16]{4,5,0,3,2,1:T(8,128)(2,1)S(1)} copy(bf16[2,16,2,4,256,16]{5,1,2,0,4,3:T(8,128)(2,1)} %bitcast.111) | data formatting | bytes 4194304 | tf_op jit(solution)/shard_map/jit(_take)/gather | solution.py:63
  193.0 12.1 %fusion.25 = (f32[16]{0:T(128)S(1)}, f32[4,16,256,16]{2,0,3,1:T(4,128)S(1)}) fusion(f32[2,16,2,4,256,16]{4,5,3,2,1,0:T(8,128)S(1)} %convolution_bitcast_fusion, f32[1,4,2,4]{1,3,0,2:T(4,128)S(1)} %copy.38, f32[1,4,2,4]{1,3,0,2:T(4,128)S(1)} %copy.37), kind=kOutput, calls=%fused_computation.44 | convolution fusion | flops 103546928 | bytes 5243200 | tf_op jit(solution)/shard_map/bcpxwn,bxeu->ecpnuw/dot_general | solution.py:68
  205.3 8.4 %all-reduce.2 = (f32[64]{0:T(128)S(1)}, f32[64]{0:T(128)S(1)}) all-reduce(f32[64]{0:T(128)S(1)} %dynamic-update-slice, f32[64]{0:T(128)S(1)} %fusion.69), channel_id=2, replica_groups=mesh['section'=4,'shard'=64] {'section'}, use_global_device_ids=true, to_apply=%add | all-reduce | flops 128 | bytes 1024
  225.9 9.0 %all-to-all-start.1 = ((bf16[16,64,224]{2,0,1:T(8,128)(2,1)}), bf16[16,64,224]{2,0,1:T(8,128)(2,1)S(1)}, u32[]{:S(2)}, u32[]{:S(2)}) async-start(bf16[16,64,224]{2,0,1:T(8,128)(2,1)} %copy.50), calls=%async_computation.1 | async-start | bytes 1048576 | tf_op jit(solution)/shard_map/all_to_all | solution.py:133
  236.9 15.6 %all-to-all-done.1 = bf16[16,64,224]{2,0,1:T(8,128)(2,1)S(1)} async-done(((bf16[16,64,224]{2,0,1:T(8,128)(2,1)}), bf16[16,64,224]{2,0,1:T(8,128)(2,1)S(1)}, u32[]{:S(2)}, u32[]{:S(2)}) %all-to-all-start.1) | async-done | bytes 458784 | tf_op jit(solution)/shard_map/all_to_all | solution.py:133
  262.8 246.6 %while.28 = (s32[]{:T(128)}, bf16[7,512,2,16]{1,3,2,0:T(8,128)(2,1)}, s32[7]{0:T(128)S(1)}, s32[1024,512]{1,0:T(8,128)}, bf16[14,1024,16]{1,2,0:T(8,128)(2,1)S(1...) while((s32[]{:T(128)}, bf16[7,512,2,16]{1,3,2,0:T(8,128)(2,1)}, s32[7]{0:T(128)S(1)}, ...), condition=%wide.region_6.7_spmd, body=%wide.region_5.6_spmd.sunk | while | flops 76611592 | bytes 13009633 | solution.py:95
  268.8 6.9 %fusion.98 = f32[512,16]{0,1:T(8,128)S(1)} fusion(f32[1024,512]{1,0:T(8,128)S(1)} %fusion.95, bf16[14,1024,16]{1,2,0:T(8,128)(2,1)S(1)} %get-tuple-element.336, s32[]{:T(128)S(6)} %select_n.175), kind=kOutput, calls=%fused_computation.19.clone.1 | convolution fusion | flops 17301504 | bytes 2162692 | tf_op jit(solution)/shard_map/while/body/eval_jaxpr/dot_general | solution.py:86
  276.9 6.9 %fusion.99 = f32[1,512,1,16]{1,3,2,0:T(8,128)S(1)} fusion(f32[512,16]{0,1:T(8,128)S(1)} %fusion.98, f32[1024,512]{1,0:T(8,128)S(1)} %fusion.95, bf16[14,1024,16]{1,2,0:T(8,128)(2,1)S(1)} %get-tuple-element.336, s32[]{:T(128)S(6)} %select_n.174), kind=kOutput, calls=%fused_computation.18.clone.1 | convolution fusion | flops 17309696 | bytes 2195460 | tf_op jit(solution)/shard_map/while/body/eval_jaxpr/dot_general | solution.py:88
  290.7 6.9 %fusion.97 = f32[1,512,1,16]{1,3,2,0:T(8,128)S(1)} fusion(f32[512,16]{0,1:T(8,128)S(1)} %fusion.96, f32[1024,512]{1,0:T(8,128)S(1)} %fusion.95, bf16[14,1024,16]{1,2,0:T(8,128)(2,1)S(1)} %get-tuple-element.336, s32[]{:T(128)S(6)} %select_n.175), kind=kOutput, calls=%fused_computation.16.clone.1 | convolution fusion | flops 17309696 | bytes 2195460 | tf_op jit(solution)/shard_map/while/body/eval_jaxpr/dot_general | solution.py:91
  304.0 6.9 %fusion.98 = f32[512,16]{0,1:T(8,128)S(1)} fusion(f32[1024,512]{1,0:T(8,128)S(1)} %fusion.95, bf16[14,1024,16]{1,2,0:T(8,128)(2,1)S(1)} %get-tuple-element.336, s32[]{:T(128)S(6)} %select_n.175), kind=kOutput, calls=%fused_computation.19.clone.1 | convolution fusion | flops 17301504 | bytes 2162692 | tf_op jit(solution)/shard_map/while/body/eval_jaxpr/dot_general | solution.py:86
  312.1 6.9 %fusion.99 = f32[1,512,1,16]{1,3,2,0:T(8,128)S(1)} fusion(f32[512,16]{0,1:T(8,128)S(1)} %fusion.98, f32[1024,512]{1,0:T(8,128)S(1)} %fusion.95, bf16[14,1024,16]{1,2,0:T(8,128)(2,1)S(1)} %get-tuple-element.336, s32[]{:T(128)S(6)} %select_n.174), kind=kOutput, calls=%fused_computation.18.clone.1 | convolution fusion | flops 17309696 | bytes 2195460 | tf_op jit(solution)/shard_map/while/body/eval_jaxpr/dot_general | solution.py:88
  325.9 6.9 %fusion.97 = f32[1,512,1,16]{1,3,2,0:T(8,128)S(1)} fusion(f32[512,16]{0,1:T(8,128)S(1)} %fusion.96, f32[1024,512]{1,0:T(8,128)S(1)} %fusion.95, bf16[14,1024,16]{1,2,0:T(8,128)(2,1)S(1)} %get-tuple-element.336, s32[]{:T(128)S(6)} %select_n.175), kind=kOutput, calls=%fused_computation.16.clone.1 | convolution fusion | flops 17309696 | bytes 2195460 | tf_op jit(solution)/shard_map/while/body/eval_jaxpr/dot_general | solution.py:91
  347.3 6.9 %fusion.99 = f32[1,512,1,16]{1,3,2,0:T(8,128)S(1)} fusion(f32[512,16]{0,1:T(8,128)S(1)} %fusion.98, f32[1024,512]{1,0:T(8,128)S(1)} %fusion.95, bf16[14,1024,16]{1,2,0:T(8,128)(2,1)S(1)} %get-tuple-element.336, s32[]{:T(128)S(6)} %select_n.174), kind=kOutput, calls=%fused_computation.18.clone.1 | convolution fusion | flops 17309696 | bytes 2195460 | tf_op jit(solution)/shard_map/while/body/eval_jaxpr/dot_general | solution.py:88
  361.1 6.9 %fusion.97 = f32[1,512,1,16]{1,3,2,0:T(8,128)S(1)} fusion(f32[512,16]{0,1:T(8,128)S(1)} %fusion.96, f32[1024,512]{1,0:T(8,128)S(1)} %fusion.95, bf16[14,1024,16]{1,2,0:T(8,128)(2,1)S(1)} %get-tuple-element.336, s32[]{:T(128)S(6)} %select_n.175), kind=kOutput, calls=%fused_computation.16.clone.1 | convolution fusion | flops 17309696 | bytes 2195460 | tf_op jit(solution)/shard_map/while/body/eval_jaxpr/dot_general | solution.py:91
  374.3 6.9 %fusion.98 = f32[512,16]{0,1:T(8,128)S(1)} fusion(f32[1024,512]{1,0:T(8,128)S(1)} %fusion.95, bf16[14,1024,16]{1,2,0:T(8,128)(2,1)S(1)} %get-tuple-element.336, s32[]{:T(128)S(6)} %select_n.175), kind=kOutput, calls=%fused_computation.19.clone.1 | convolution fusion | flops 17301504 | bytes 2162692 | tf_op jit(solution)/shard_map/while/body/eval_jaxpr/dot_general | solution.py:86
  382.5 6.9 %fusion.99 = f32[1,512,1,16]{1,3,2,0:T(8,128)S(1)} fusion(f32[512,16]{0,1:T(8,128)S(1)} %fusion.98, f32[1024,512]{1,0:T(8,128)S(1)} %fusion.95, bf16[14,1024,16]{1,2,0:T(8,128)(2,1)S(1)} %get-tuple-element.336, s32[]{:T(128)S(6)} %select_n.174), kind=kOutput, calls=%fused_computation.18.clone.1 | convolution fusion | flops 17309696 | bytes 2195460 | tf_op jit(solution)/shard_map/while/body/eval_jaxpr/dot_general | solution.py:88
  396.3 6.9 %fusion.97 = f32[1,512,1,16]{1,3,2,0:T(8,128)S(1)} fusion(f32[512,16]{0,1:T(8,128)S(1)} %fusion.96, f32[1024,512]{1,0:T(8,128)S(1)} %fusion.95, bf16[14,1024,16]{1,2,0:T(8,128)(2,1)S(1)} %get-tuple-element.336, s32[]{:T(128)S(6)} %select_n.175), kind=kOutput, calls=%fused_computation.16.clone.1 | convolution fusion | flops 17309696 | bytes 2195460 | tf_op jit(solution)/shard_map/while/body/eval_jaxpr/dot_general | solution.py:91
  417.7 6.9 %fusion.99 = f32[1,512,1,16]{1,3,2,0:T(8,128)S(1)} fusion(f32[512,16]{0,1:T(8,128)S(1)} %fusion.98, f32[1024,512]{1,0:T(8,128)S(1)} %fusion.95, bf16[14,1024,16]{1,2,0:T(8,128)(2,1)S(1)} %get-tuple-element.336, s32[]{:T(128)S(6)} %select_n.174), kind=kOutput, calls=%fused_computation.18.clone.1 | convolution fusion | flops 17309696 | bytes 2195460 | tf_op jit(solution)/shard_map/while/body/eval_jaxpr/dot_general | solution.py:88
  431.5 6.9 %fusion.97 = f32[1,512,1,16]{1,3,2,0:T(8,128)S(1)} fusion(f32[512,16]{0,1:T(8,128)S(1)} %fusion.96, f32[1024,512]{1,0:T(8,128)S(1)} %fusion.95, bf16[14,1024,16]{1,2,0:T(8,128)(2,1)S(1)} %get-tuple-element.336, s32[]{:T(128)S(6)} %select_n.175), kind=kOutput, calls=%fused_computation.16.clone.1 | convolution fusion | flops 17309696 | bytes 2195460 | tf_op jit(solution)/shard_map/while/body/eval_jaxpr/dot_general | solution.py:91
  452.9 6.9 %fusion.99 = f32[1,512,1,16]{1,3,2,0:T(8,128)S(1)} fusion(f32[512,16]{0,1:T(8,128)S(1)} %fusion.98, f32[1024,512]{1,0:T(8,128)S(1)} %fusion.95, bf16[14,1024,16]{1,2,0:T(8,128)(2,1)S(1)} %get-tuple-element.336, s32[]{:T(128)S(6)} %select_n.174), kind=kOutput, calls=%fused_computation.18.clone.1 | convolution fusion | flops 17309696 | bytes 2195460 | tf_op jit(solution)/shard_map/while/body/eval_jaxpr/dot_general | solution.py:88
  466.7 6.9 %fusion.97 = f32[1,512,1,16]{1,3,2,0:T(8,128)S(1)} fusion(f32[512,16]{0,1:T(8,128)S(1)} %fusion.96, f32[1024,512]{1,0:T(8,128)S(1)} %fusion.95, bf16[14,1024,16]{1,2,0:T(8,128)(2,1)S(1)} %get-tuple-element.336, s32[]{:T(128)S(6)} %select_n.175), kind=kOutput, calls=%fused_computation.16.clone.1 | convolution fusion | flops 17309696 | bytes 2195460 | tf_op jit(solution)/shard_map/while/body/eval_jaxpr/dot_general | solution.py:91
  488.1 6.9 %fusion.99 = f32[1,512,1,16]{1,3,2,0:T(8,128)S(1)} fusion(f32[512,16]{0,1:T(8,128)S(1)} %fusion.98, f32[1024,512]{1,0:T(8,128)S(1)} %fusion.95, bf16[14,1024,16]{1,2,0:T(8,128)(2,1)S(1)} %get-tuple-element.336, s32[]{:T(128)S(6)} %select_n.174), kind=kOutput, calls=%fused_computation.18.clone.1 | convolution fusion | flops 17309696 | bytes 2195460 | tf_op jit(solution)/shard_map/while/body/eval_jaxpr/dot_general | solution.py:88
  501.9 6.9 %fusion.97 = f32[1,512,1,16]{1,3,2,0:T(8,128)S(1)} fusion(f32[512,16]{0,1:T(8,128)S(1)} %fusion.96, f32[1024,512]{1,0:T(8,128)S(1)} %fusion.95, bf16[14,1024,16]{1,2,0:T(8,128)(2,1)S(1)} %get-tuple-element.336, s32[]{:T(128)S(6)} %select_n.175), kind=kOutput, calls=%fused_computation.16.clone.1 | convolution fusion | flops 17309696 | bytes 2195460 | tf_op jit(solution)/shard_map/while/body/eval_jaxpr/dot_general | solution.py:91
  (95 shorter events, 159.9 us)
Async XLA Ops:
  17.4 13.3 %copy-start.2 = (bf16[2,16,1024]{2,1,0:T(8,128)(2,1)S(1)}, bf16[2,16,1024]{2,1,0:T(8,128)(2,1)}, u32[]{:S(2)}) copy-start(bf16[2,16,1024]{2,1,0:T(8,128)(2,1)} %param.11) | copy-start | bytes 196612
  17.4 13.3 %copy-start.3 = (s32[1024]{0:T(1024)S(1)}, s32[1024]{0:T(1024)}, u32[]{:S(2)}) copy-start(s32[1024]{0:T(1024)} %param.12) | copy-start | bytes 12292
  17.4 18.5 %copy-start.5 = (u32[256]{0:T(256)S(1)}, u32[256]{0:T(256)}, u32[]{:S(2)}) copy-start(u32[256]{0:T(256)} %constant.192) | copy-start | bytes 3076
  17.4 19.9 %copy-start.4 = (f32[16]{0:T(128)S(1)}, f32[16]{0:T(128)}, u32[]{:S(2)}) copy-start(f32[16]{0:T(128)} %param.13) | copy-start | bytes 196
  17.4 63.0 %all-to-all-start = ((bf16[2,1024,2,256]{3,2,0,1:T(2,128)(2,1)}), bf16[2,1024,2,256]{3,2,0,1:T(2,128)(2,1)S(1)}, u32[]{:S(2)}, u32[]{:S(2)}) async-start(bf16[2,1024,2,256]{3,2,0,1:T(2,128)(2,1)} %copy.40), calls=%async_computation | async-start | bytes 4194304 | tf_op jit(solution)/shard_map/all_to_all | solution.py:120
  174.6 17.1 %copy-start.1 = (bf16[1,256,2,256]{3,1,0,2:T(8,128)(2,1)S(1)}, bf16[1,256,2,256]{3,1,0,2:T(8,128)(2,1)}, u32[]{:S(2)}) copy-start(bf16[1,256,2,256]{3,1,0,2:T(8,128)(2,1)} %get-tuple-element.201) | copy-start | bytes 786436
  224.8 10.1 %copy-start = (s32[1024,512]{1,0:T(8,128)S(1)}, s32[1024,512]{1,0:T(8,128)}, u32[]{:S(2)}) copy-start(s32[1024,512]{1,0:T(8,128)} %param.14) | copy-start | bytes 6291460
  225.9 26.7 %all-to-all-start.1 = ((bf16[16,64,224]{2,0,1:T(8,128)(2,1)}), bf16[16,64,224]{2,0,1:T(8,128)(2,1)S(1)}, u32[]{:S(2)}, u32[]{:S(2)}) async-start(bf16[16,64,224]{2,0,1:T(8,128)(2,1)} %copy.50), calls=%async_computation.1 | async-start | bytes 1048576 | tf_op jit(solution)/shard_map/all_to_all | solution.py:133
where the time goes:
time: 516 us; the launch traced here: 510 us
  matrix products  217 us (42%)
  local copies, waits for them, and re-layouts  131 us (25%)
  waiting for transfers between devices  55.5 us (11%)
  other arithmetic  47.6 us (9%)
  loops' own time  27.1 us (5%)
  starting transfers between devices  22.3 us (4%)
  blocking collectives  8.44 us (2%)
    dot_general x7, matrix products, per_frequency(): lax.dot_general(sine_part, mod_imag, contract, preferred_element_type=jnp...  48.5 us
    dot_general x7, matrix products, per_frequency(): lax.dot_general(sine_part, mod_real, contract, preferred_element_type=jnp...  48.4 us
    dot_general x7, matrix products, per_frequency(): lax.dot_general(cosine_part, mod_real, contract, preferred_element_type=j...  48.1 us
    dot_general x7, matrix products, per_frequency(): lax.dot_general(cosine_part, mod_imag, contract, preferred_element_type=j...  48 us
    all_to_all x1, waiting for transfers between devices, shards(): lax.all_to_all(spectra, 'shard', split_axis=1, concat_axis=3, tiled=True)  39.9 us
    gather x2, local copies, waits for them, and re-layouts, form_beams(): jnp.take(calibrated, cell_feed, axis=3)  37.3 us
    another operation x1, loops' own time, dedisperse(): return lax.map(per_frequency, jnp.arange(MODF, dtype=jnp.int32))  27.1 us
    slice x5, local copies, waits for them, and re-layouts, form_beams(): real_part = gain_values[0] * values[0] - gain_values[1] * values[1]  23.2 us
  transfers between devices with their start and end apart: 2, of which 2 were waited for; matrix products, arithmetic and copies ran while one was open for 2% of the time, Pallas kernels for 0%

commit v1 on v0

--- a/solution.py
+++ b/solution.py
@@ -130,7 +130,12 @@
         "cnb,nq->cbq", normalized, frame_table(), precision=lax.Precision.HIGHEST
     ).astype(jnp.bfloat16)
     flattened = modulated.reshape(modulated.shape[0], FEEDS * 2 * MODF)
-    moved = lax.all_to_all(flattened, "shard", split_axis=1, concat_axis=0, tiled=True)
+    moved = jnp.concatenate(
+        lax.all_to_all(
+            jnp.stack(jnp.split(flattened, lax.axis_size("shard"), axis=1)), "shard", 0, 0
+        ),
+        axis=0,
+    )
     local_beams = FEEDS // lax.axis_size("shard")
     gathered = moved.reshape(CHANS, local_beams, 2 * MODF)
     freq_major = jnp.transpose(gathered, (2, 0, 1))

time: 516 us -> 560 us (1.085)
  local copies, waits for them, and re-layouts: 131 us -> 175 us
    unnamed x16 -> x79, local copies, waits for them, and re-layouts: 0.93 us -> 41.9 us
    another operation x2 -> x4, local copies, waits for them, and re-layouts: 0.01 us -> 7.34 us  [the longest x1 6.67 us: shards(): gathered = moved.reshape(CHANS, local_beams, 2 * MODF)]
    all_to_all x3 -> x1, local copies, waits for them, and re-layouts: 10.3 us -> 3.34 us  [shards(): lax.all_to_all(jnp.stack(jnp.split(flattened, lax.axis_size('shard'), axi...]
where the time goes in v1:
time: 560 us; the launch traced here: 554 us
  matrix products  217 us (39%)
  local copies, waits for them, and re-layouts  175 us (31%)
  waiting for transfers between devices  55.5 us (10%)
  other arithmetic  47.6 us (8%)
  loops' own time  27.1 us (5%)
  starting transfers between devices  22.3 us (4%)
  blocking collectives  8.44 us (2%)
    dot_general x7, matrix products, per_frequency(): lax.dot_general(sine_part, mod_imag, contract, preferred_element_type=jnp...  48.5 us
    dot_general x7, matrix products, per_frequency(): lax.dot_general(sine_part, mod_real, contract, preferred_element_type=jnp...  48.4 us
    dot_general x7, matrix products, per_frequency(): lax.dot_general(cosine_part, mod_real, contract, preferred_element_type=j...  48.1 us
    dot_general x7, matrix products, per_frequency(): lax.dot_general(cosine_part, mod_imag, contract, preferred_element_type=j...  48 us
    unnamed x79, local copies, waits for them, and re-layouts  41.9 us
    all_to_all x1, waiting for transfers between devices, shards(): lax.all_to_all(spectra, 'shard', split_axis=1, concat_axis=3, tiled=True)  39.9 us
    gather x2, local copies, waits for them, and re-layouts, form_beams(): jnp.take(calibrated, cell_feed, axis=3)  37.3 us
    another operation x1, loops' own time, dedisperse(): return lax.map(per_frequency, jnp.arange(MODF, dtype=jnp.int32))  27.1 us
  transfers between devices with their start and end apart: 2, of which 2 were waited for; matrix products, arithmetic and copies ran while one was open for 2% of the time, Pallas kernels for 0%

profile of v1, /device:TPU:1, one launch (start us, length us, event | category | flops | bytes accessed | tf_op | source)
XLA Modules:
  0.0 553.6 jit_solution(8334325291202764214)
XLA Ops:
  2.9 9.2 %multiply_convert_fusion = bf16[2048,512]{1,0:T(8,128)(2,1)} fusion(bf16[2048,2048]{1,0:T(8,128)(2,1)} %constant.189, bf16[512,2048]{1,0:T(8,128)(2,1)S(1)} %reshape_squeeze.3), kind=kOutput, calls=%fused_computation.43 | convolution fusion | flops 4297064448 | bytes 12582912 | tf_op jit(solution)/shard_map/dot_general | solution.py:112
  17.4 13.3 %all-to-all-start = ((bf16[2,1024,2,256]{3,2,0,1:T(2,128)(2,1)}), bf16[2,1024,2,256]{3,2,0,1:T(2,128)(2,1)S(1)}, u32[]{:S(2)}, u32[]{:S(2)}) async-start(bf16[2,1024,2,256]{3,2,0,1:T(2,128)(2,1)} %copy.40), calls=%async_computation | async-start | bytes 4194304 | tf_op jit(solution)/shard_map/all_to_all | solution.py:120
  40.5 39.9 %all-to-all-done = bf16[2,1024,2,256]{3,2,0,1:T(2,128)(2,1)S(1)} async-done(((bf16[2,1024,2,256]{3,2,0,1:T(2,128)(2,1)}), bf16[2,1024,2,256]{3,2,0,1:T(2,128)(2,1)S(1)}, u32[]{:S(2)}, u32[]{:S(2)}) %all-to-all-start) | async-done | bytes 2097184 | tf_op jit(solution)/shard_map/all_to_all | solution.py:120
  84.5 8.6 %slice.26 = f32[1,16,2,1024,16]{4,3,2,1,0:T(8,128)} reshape(f32[1,16,2,64,256]{4,3,2,1,0:T(8,128)S(1)} %copy.42) | data formatting | bytes 4194304 | tf_op jit(solution)/shard_map/slice | solution.py:60
  95.9 8.6 %slice.29 = f32[1,16,2,1024,16]{4,3,2,1,0:T(8,128)} reshape(f32[1,16,2,64,256]{4,3,2,1,0:T(8,128)S(1)} %copy.43) | data formatting | bytes 4194304 | tf_op jit(solution)/shard_map/slice | solution.py:60
  104.5 18.1 %multiply_subtract_fusion = (bf16[1,16,2,1024,16]{4,3,2,1,0:T(8,128)(2,1)}, bf16[1,16,2,1024,16]{4,3,2,1,0:T(8,128)(2,1)}) fusion(f32[1,16,2,1024,16]{4,3,2,1,0:T(8,128)} %slice.29, f32[1,16,2,1024,16]{4,3,2,1,0:T(8,128)} %slice.26, f32[16,1024]{1,0:T(8,128)S(1)} %get-tuple-element.203, f32[16,1024]{1,0:T(8,128)S(1)} %get-tuple-element.202), kind=kLoop, calls=%fused_computation.37 | loop fusion | flops 4194304 | bytes 6422528 | tf_op jit(solution)/shard_map/sub | solution.py:60
  129.2 7.8 %copy.45 = bf16[1,16,2,1024,16]{3,4,2,1,0:T(8,128)(2,1)} copy(bf16[1,16,2,1024,16]{4,3,2,1,0:T(8,128)(2,1)} %get-tuple-element.197) | data formatting | bytes 2097152 | tf_op jit(solution)/shard_map/add | solution.py:61
  138.4 16.1 %copy.46 = bf16[2,16,2,1024,16]{4,1,3,2,0:T(8,128)(2,1)} copy(bf16[2,16,2,1024,16]{3,4,2,1,0:T(8,128)(2,1)S(1)} %pad_maximum_fusion) | data formatting | bytes 4194304 | tf_op jit(solution)/shard_map/stack | solution.py:62
  154.5 20.1 %gather_fusion = bf16[1024,2,16,2,16]{4,2,3,1,0:T(8,128)(2,1)} fusion(bf16[2,16,2,1024,16]{4,1,3,2,0:T(8,128)(2,1)} %copy.46, s32[1024]{0:T(1024)S(1)} %fusion.59), kind=kCustom, calls=%fused_computation | custom fusion | bytes 4198400 | tf_op jit(solution)/shard_map/jit(_take)/gather | solution.py:63
  174.7 17.1 %copy.47 = bf16[2,16,2,4,256,16]{4,5,0,3,2,1:T(8,128)(2,1)S(1)} copy(bf16[2,16,2,4,256,16]{5,1,2,0,4,3:T(8,128)(2,1)} %bitcast.366) | data formatting | bytes 4194304 | tf_op jit(solution)/shard_map/jit(_take)/gather | solution.py:63
  193.0 12.1 %fusion.25 = (f32[16]{0:T(128)S(1)}, f32[4,16,256,16]{2,0,3,1:T(4,128)S(1)}) fusion(f32[2,16,2,4,256,16]{4,5,3,2,1,0:T(8,128)S(1)} %convolution_bitcast_fusion, f32[1,4,2,4]{1,3,0,2:T(4,128)S(1)} %copy.38, f32[1,4,2,4]{1,3,0,2:T(4,128)S(1)} %copy.37), kind=kOutput, calls=%fused_computation.44 | convolution fusion | flops 103546928 | bytes 5243200 | tf_op jit(solution)/shard_map/bcpxwn,bxeu->ecpnuw/dot_general | solution.py:68
  205.3 8.4 %all-reduce.2 = (f32[64]{0:T(128)S(1)}, f32[64]{0:T(128)S(1)}) all-reduce(f32[64]{0:T(128)S(1)} %dynamic-update-slice, f32[64]{0:T(128)S(1)} %fusion.69), channel_id=2, replica_groups=mesh['section'=4,'shard'=64] {'section'}, use_global_device_ids=true, to_apply=%add | all-reduce | flops 128 | bytes 1024
  218.9 9.0 %reshape.240 = bf16[16,14336]{1,0:T(8,128)(2,1)S(1)} reshape(bf16[16,1024,14]{2,1,0:T(8,128)(2,1)} %copy.49) | data formatting | bytes 917504 | tf_op jit(solution)/shard_map/reshape | solution.py:132
  269.7 9.0 %all-to-all-start.1 = ((bf16[64,16,224]{2,1,0:T(8,128)(2,1)}), bf16[64,16,224]{2,1,0:T(8,128)(2,1)S(1)}, u32[]{:S(2)}, u32[]{:S(2)}) async-start(bf16[64,16,224]{2,1,0:T(8,128)(2,1)} %constant_dynamic-update-slice_fusion), calls=%async_computation.1 | async-start | bytes 1048576 | tf_op jit(solution)/shard_map/all_to_all | solution.py:134
  280.8 15.6 %all-to-all-done.1 = bf16[64,16,224]{2,1,0:T(8,128)(2,1)S(1)} async-done(((bf16[64,16,224]{2,1,0:T(8,128)(2,1)}), bf16[64,16,224]{2,1,0:T(8,128)(2,1)S(1)}, u32[]{:S(2)}, u32[]{:S(2)}) %all-to-all-start.1) | async-done | bytes 458784 | tf_op jit(solution)/shard_map/all_to_all | solution.py:134
  306.7 246.6 %while.28 = (s32[]{:T(128)}, bf16[7,512,2,16]{1,3,2,0:T(8,128)(2,1)}, s32[7]{0:T(128)S(1)}, s32[1024,512]{1,0:T(8,128)}, bf16[14,1024,16]{1,2,0:T(8,128)(2,1)S(1...) while((s32[]{:T(128)}, bf16[7,512,2,16]{1,3,2,0:T(8,128)(2,1)}, s32[7]{0:T(128)S(1)}, ...), condition=%wide.region_6.7_spmd, body=%wide.region_5.6_spmd.sunk | while | flops 76611592 | bytes 13009633 | solution.py:95
  312.6 6.9 %fusion.98 = f32[512,16]{0,1:T(8,128)S(1)} fusion(f32[1024,512]{1,0:T(8,128)S(1)} %fusion.95, bf16[14,1024,16]{1,2,0:T(8,128)(2,1)S(1)} %get-tuple-element.336, s32[]{:T(128)S(6)} %select_n.175), kind=kOutput, calls=%fused_computation.19.clone.1 | convolution fusion | flops 17301504 | bytes 2162692 | tf_op jit(solution)/shard_map/while/body/eval_jaxpr/dot_general | solution.py:86
  320.8 6.9 %fusion.99 = f32[1,512,1,16]{1,3,2,0:T(8,128)S(1)} fusion(f32[512,16]{0,1:T(8,128)S(1)} %fusion.98, f32[1024,512]{1,0:T(8,128)S(1)} %fusion.95, bf16[14,1024,16]{1,2,0:T(8,128)(2,1)S(1)} %get-tuple-element.336, s32[]{:T(128)S(6)} %select_n.174), kind=kOutput, calls=%fused_computation.18.clone.1 | convolution fusion | flops 17309696 | bytes 2195460 | tf_op jit(solution)/shard_map/while/body/eval_jaxpr/dot_general | solution.py:88
  334.5 6.9 %fusion.97 = f32[1,512,1,16]{1,3,2,0:T(8,128)S(1)} fusion(f32[512,16]{0,1:T(8,128)S(1)} %fusion.96, f32[1024,512]{1,0:T(8,128)S(1)} %fusion.95, bf16[14,1024,16]{1,2,0:T(8,128)(2,1)S(1)} %get-tuple-element.336, s32[]{:T(128)S(6)} %select_n.175), kind=kOutput, calls=%fused_computation.16.clone.1 | convolution fusion | flops 17309696 | bytes 2195460 | tf_op jit(solution)/shard_map/while/body/eval_jaxpr/dot_general | solution.py:91
  356.0 6.9 %fusion.99 = f32[1,512,1,16]{1,3,2,0:T(8,128)S(1)} fusion(f32[512,16]{0,1:T(8,128)S(1)} %fusion.98, f32[1024,512]{1,0:T(8,128)S(1)} %fusion.95, bf16[14,1024,16]{1,2,0:T(8,128)(2,1)S(1)} %get-tuple-element.336, s32[]{:T(128)S(6)} %select_n.174), kind=kOutput, calls=%fused_computation.18.clone.1 | convolution fusion | flops 17309696 | bytes 2195460 | tf_op jit(solution)/shard_map/while/body/eval_jaxpr/dot_general | solution.py:88
  369.7 6.9 %fusion.97 = f32[1,512,1,16]{1,3,2,0:T(8,128)S(1)} fusion(f32[512,16]{0,1:T(8,128)S(1)} %fusion.96, f32[1024,512]{1,0:T(8,128)S(1)} %fusion.95, bf16[14,1024,16]{1,2,0:T(8,128)(2,1)S(1)} %get-tuple-element.336, s32[]{:T(128)S(6)} %select_n.175), kind=kOutput, calls=%fused_computation.16.clone.1 | convolution fusion | flops 17309696 | bytes 2195460 | tf_op jit(solution)/shard_map/while/body/eval_jaxpr/dot_general | solution.py:91
  383.0 6.9 %fusion.98 = f32[512,16]{0,1:T(8,128)S(1)} fusion(f32[1024,512]{1,0:T(8,128)S(1)} %fusion.95, bf16[14,1024,16]{1,2,0:T(8,128)(2,1)S(1)} %get-tuple-element.336, s32[]{:T(128)S(6)} %select_n.175), kind=kOutput, calls=%fused_computation.19.clone.1 | convolution fusion | flops 17301504 | bytes 2162692 | tf_op jit(solution)/shard_map/while/body/eval_jaxpr/dot_general | solution.py:86
  391.1 6.9 %fusion.99 = f32[1,512,1,16]{1,3,2,0:T(8,128)S(1)} fusion(f32[512,16]{0,1:T(8,128)S(1)} %fusion.98, f32[1024,512]{1,0:T(8,128)S(1)} %fusion.95, bf16[14,1024,16]{1,2,0:T(8,128)(2,1)S(1)} %get-tuple-element.336, s32[]{:T(128)S(6)} %select_n.174), kind=kOutput, calls=%fused_computation.18.clone.1 | convolution fusion | flops 17309696 | bytes 2195460 | tf_op jit(solution)/shard_map/while/body/eval_jaxpr/dot_general | solution.py:88
  404.9 6.9 %fusion.97 = f32[1,512,1,16]{1,3,2,0:T(8,128)S(1)} fusion(f32[512,16]{0,1:T(8,128)S(1)} %fusion.96, f32[1024,512]{1,0:T(8,128)S(1)} %fusion.95, bf16[14,1024,16]{1,2,0:T(8,128)(2,1)S(1)} %get-tuple-element.336, s32[]{:T(128)S(6)} %select_n.175), kind=kOutput, calls=%fused_computation.16.clone.1 | convolution fusion | flops 17309696 | bytes 2195460 | tf_op jit(solution)/shard_map/while/body/eval_jaxpr/dot_general | solution.py:91
  426.3 6.9 %fusion.99 = f32[1,512,1,16]{1,3,2,0:T(8,128)S(1)} fusion(f32[512,16]{0,1:T(8,128)S(1)} %fusion.98, f32[1024,512]{1,0:T(8,128)S(1)} %fusion.95, bf16[14,1024,16]{1,2,0:T(8,128)(2,1)S(1)} %get-tuple-element.336, s32[]{:T(128)S(6)} %select_n.174), kind=kOutput, calls=%fused_computation.18.clone.1 | convolution fusion | flops 17309696 | bytes 2195460 | tf_op jit(solution)/shard_map/while/body/eval_jaxpr/dot_general | solution.py:88
  440.1 6.9 %fusion.97 = f32[1,512,1,16]{1,3,2,0:T(8,128)S(1)} fusion(f32[512,16]{0,1:T(8,128)S(1)} %fusion.96, f32[1024,512]{1,0:T(8,128)S(1)} %fusion.95, bf16[14,1024,16]{1,2,0:T(8,128)(2,1)S(1)} %get-tuple-element.336, s32[]{:T(128)S(6)} %select_n.175), kind=kOutput, calls=%fused_computation.16.clone.1 | convolution fusion | flops 17309696 | bytes 2195460 | tf_op jit(solution)/shard_map/while/body/eval_jaxpr/dot_general | solution.py:91
  461.5 6.9 %fusion.99 = f32[1,512,1,16]{1,3,2,0:T(8,128)S(1)} fusion(f32[512,16]{0,1:T(8,128)S(1)} %fusion.98, f32[1024,512]{1,0:T(8,128)S(1)} %fusion.95, bf16[14,1024,16]{1,2,0:T(8,128)(2,1)S(1)} %get-tuple-element.336, s32[]{:T(128)S(6)} %select_n.174), kind=kOutput, calls=%fused_computation.18.clone.1 | convolution fusion | flops 17309696 | bytes 2195460 | tf_op jit(solution)/shard_map/while/body/eval_jaxpr/dot_general | solution.py:88
  475.3 6.9 %fusion.97 = f32[1,512,1,16]{1,3,2,0:T(8,128)S(1)} fusion(f32[512,16]{0,1:T(8,128)S(1)} %fusion.96, f32[1024,512]{1,0:T(8,128)S(1)} %fusion.95, bf16[14,1024,16]{1,2,0:T(8,128)(2,1)S(1)} %get-tuple-element.336, s32[]{:T(128)S(6)} %select_n.175), kind=kOutput, calls=%fused_computation.16.clone.1 | convolution fusion | flops 17309696 | bytes 2195460 | tf_op jit(solution)/shard_map/while/body/eval_jaxpr/dot_general | solution.py:91
  496.7 6.9 %fusion.99 = f32[1,512,1,16]{1,3,2,0:T(8,128)S(1)} fusion(f32[512,16]{0,1:T(8,128)S(1)} %fusion.98, f32[1024,512]{1,0:T(8,128)S(1)} %fusion.95, bf16[14,1024,16]{1,2,0:T(8,128)(2,1)S(1)} %get-tuple-element.336, s32[]{:T(128)S(6)} %select_n.174), kind=kOutput, calls=%fused_computation.18.clone.1 | convolution fusion | flops 17309696 | bytes 2195460 | tf_op jit(solution)/shard_map/while/body/eval_jaxpr/dot_general | solution.py:88
  510.5 6.9 %fusion.97 = f32[1,512,1,16]{1,3,2,0:T(8,128)S(1)} fusion(f32[512,16]{0,1:T(8,128)S(1)} %fusion.96, f32[1024,512]{1,0:T(8,128)S(1)} %fusion.95, bf16[14,1024,16]{1,2,0:T(8,128)(2,1)S(1)} %get-tuple-element.336, s32[]{:T(128)S(6)} %select_n.175), kind=kOutput, calls=%fused_computation.16.clone.1 | convolution fusion | flops 17309696 | bytes 2195460 | tf_op jit(solution)/shard_map/while/body/eval_jaxpr/dot_general | solution.py:91
  531.9 6.9 %fusion.99 = f32[1,512,1,16]{1,3,2,0:T(8,128)S(1)} fusion(f32[512,16]{0,1:T(8,128)S(1)} %fusion.98, f32[1024,512]{1,0:T(8,128)S(1)} %fusion.95, bf16[14,1024,16]{1,2,0:T(8,128)(2,1)S(1)} %get-tuple-element.336, s32[]{:T(128)S(6)} %select_n.174), kind=kOutput, calls=%fused_computation.18.clone.1 | convolution fusion | flops 17309696 | bytes 2195460 | tf_op jit(solution)/shard_map/while/body/eval_jaxpr/dot_general | solution.py:88
  545.7 6.9 %fusion.97 = f32[1,512,1,16]{1,3,2,0:T(8,128)S(1)} fusion(f32[512,16]{0,1:T(8,128)S(1)} %fusion.96, f32[1024,512]{1,0:T(8,128)S(1)} %fusion.95, bf16[14,1024,16]{1,2,0:T(8,128)(2,1)S(1)} %get-tuple-element.336, s32[]{:T(128)S(6)} %select_n.175), kind=kOutput, calls=%fused_computation.16.clone.1 | convolution fusion | flops 17309696 | bytes 2195460 | tf_op jit(solution)/shard_map/while/body/eval_jaxpr/dot_general | solution.py:91
  (158 shorter events, 201.5 us)
Async XLA Ops:
  17.4 13.3 %copy-start.2 = (bf16[2,16,1024]{2,1,0:T(8,128)(2,1)S(1)}, bf16[2,16,1024]{2,1,0:T(8,128)(2,1)}, u32[]{:S(2)}) copy-start(bf16[2,16,1024]{2,1,0:T(8,128)(2,1)} %param.11) | copy-start | bytes 196612
  17.4 13.3 %copy-start.3 = (s32[1024]{0:T(1024)S(1)}, s32[1024]{0:T(1024)}, u32[]{:S(2)}) copy-start(s32[1024]{0:T(1024)} %param.12) | copy-start | bytes 12292
  17.4 18.5 %copy-start.5 = (u32[256]{0:T(256)S(1)}, u32[256]{0:T(256)}, u32[]{:S(2)}) copy-start(u32[256]{0:T(256)} %constant.192) | copy-start | bytes 3076
  17.4 19.9 %copy-start.4 = (f32[16]{0:T(128)S(1)}, f32[16]{0:T(128)}, u32[]{:S(2)}) copy-start(f32[16]{0:T(128)} %param.13) | copy-start | bytes 196
  17.4 63.0 %all-to-all-start = ((bf16[2,1024,2,256]{3,2,0,1:T(2,128)(2,1)}), bf16[2,1024,2,256]{3,2,0,1:T(2,128)(2,1)S(1)}, u32[]{:S(2)}, u32[]{:S(2)}) async-start(bf16[2,1024,2,256]{3,2,0,1:T(2,128)(2,1)} %copy.40), calls=%async_computation | async-start | bytes 4194304 | tf_op jit(solution)/shard_map/all_to_all | solution.py:120
  174.6 17.1 %copy-start.1 = (bf16[1,256,2,256]{3,1,0,2:T(8,128)(2,1)S(1)}, bf16[1,256,2,256]{3,1,0,2:T(8,128)(2,1)}, u32[]{:S(2)}) copy-start(bf16[1,256,2,256]{3,1,0,2:T(8,128)(2,1)} %get-tuple-element.201) | copy-start | bytes 786436
  228.0 50.7 %copy-start = (s32[1024,512]{1,0:T(8,128)S(1)}, s32[1024,512]{1,0:T(8,128)}, u32[]{:S(2)}) copy-start(s32[1024,512]{1,0:T(8,128)} %param.14) | copy-start | bytes 6291460
  269.7 26.7 %all-to-all-start.1 = ((bf16[64,16,224]{2,1,0:T(8,128)(2,1)}), bf16[64,16,224]{2,1,0:T(8,128)(2,1)S(1)}, u32[]{:S(2)}, u32[]{:S(2)}) async-start(bf16[64,16,224]{2,1,0:T(8,128)(2,1)} %constant_dynamic-update-slice_fusion), calls=%async_computation.1 | async-start | bytes 1048576 | tf_op jit(solution)/shard_map/all_to_all | solution.py:134
